TPU v7x, 128 devices: a whole 4x4x4 slice. The times are simulated.
128 devices in a mesh: sx: 8 (over y, core), sy: 16 (over x, z).
Axes of the slice: x: 4, y: 4, z: 4, core: 2. Of those that a mesh axis runs over, the one named last changes fastest.
Arguments:
- loads: float32 [8, 16, 1536, 256], P('sx', 'sy')
- schur_flex: float32 [8, 16, 1536, 1536], P('sx', 'sy'), as said below
- dirichlet: float32 [8, 16, 1536, 1536], P('sx', 'sy'), as said below
- coupling: float32 [8, 16, 16, 1536], P('sx', 'sy'), may hold values from -0.3125 to 0.3125
- corner_index: int32 [8, 16, 16], P('sx', 'sy'), may hold values from 0 to 512, as said below
- face_lists: int32 [8, 16, 4, 384], P('sx', 'sy'), may hold values from 0 to 383, as said below
- coarse_inverse: float32 [512, 512], P(('sx', 'sy')), as said below
Outputs:
- multipliers: float32 [8, 16, 1536, 256], P('sx', 'sy')
- residual: float32 [8, 16, 1536, 256], P('sx', 'sy')
Inputs may be any that keep to these rules, and one draw needn't show every extreme that they name: `corner_index`: each subdomain lists 4 coarse dofs for each of its four corners; 512 marks a corner on the clamped edges of the panel, which has no coarse dof; every coarse dof below 512 is named by some subdomain. `face_lists`: each face's list is a permutation of the 384 dofs of the facing face; the facing lists of two neighbouring subdomains are inverse permutations. `schur_flex`: symmetric positive definite for every subdomain. `dirichlet`: symmetric positive definite for every subdomain. `coarse_inverse`: symmetric positive definite.
All inputs are finite; a program needn't handle non-finite values.
Results may differ from a plain program's by a relative error of at most 0.00017.
Values sent between devices are 32-bit elements; how exact they have to be, the bound alone decides.
A program may use at most 128 MiB of HBM per device.

v0:
```python
import jax
import jax.numpy as jnp
from jax import lax
from jax.sharding import PartitionSpec as P

ITERS = 2


def shifted(block, axis, distance):
    devices = range(lax.axis_size(axis))
    route = [(i - distance, i) for i in devices if i - distance in devices]
    return lax.ppermute(block, axis, route)


def jump(field, face_index):
    size = field.shape[0] // 4
    width = field.shape[1]
    face_rows = field.reshape(4, size, width)
    from_low_x = shifted(face_rows[1], "sx", 1)
    from_high_x = shifted(face_rows[0], "sx", -1)
    from_low_y = shifted(face_rows[3], "sy", 1)
    from_high_y = shifted(face_rows[2], "sy", -1)
    received = jnp.stack([from_low_x, from_high_x, from_low_y, from_high_y], axis=0)
    matched = received[jnp.arange(4, dtype=jnp.int32)[:, None], face_index]
    return (face_rows - matched).reshape(4 * size, width)


def coarse_solve(coarse_rhs, stiffness_inverse_lines):
    highest = lax.Precision.HIGHEST
    total = lax.psum(coarse_rhs, ("sx", "sy"))
    mine = jnp.dot(stiffness_inverse_lines, total, precision=highest)
    return lax.all_gather(mine, ("sx", "sy"), axis=0, tiled=True)


def inner(first, second):
    return jnp.sum(first * second, axis=0)


def shards(loads, schur_flex, dirichlet, coupling, corner_index, face_lists, coarse_inverse):
    highest = lax.Precision.HIGHEST
    flex_mat = schur_flex[0, 0]
    prec_mat = dirichlet[0, 0]
    coupling_mat = coupling[0, 0]
    corners = corner_index[0, 0]
    face_index = face_lists[0, 0]
    ncoarse = coarse_inverse.shape[1]
    onehot = (corners[None, :] == jnp.arange(ncoarse, dtype=jnp.int32)[:, None]).astype(jnp.float32)

    def precondition(dual_vector):
        spread = jump(dual_vector, face_index)
        operator_applied = jnp.dot(prec_mat, spread, precision=highest)
        return 0.5 * jump(operator_applied, face_index)

    def residual_dot(residual, precond):
        return lax.psum(inner(residual, precond), ("sx", "sy"))

    force_discontinuity = jump(loads[0, 0], face_index)
    multipliers = jnp.zeros_like(force_discontinuity)
    residual = force_discontinuity
    precond = precondition(residual)
    direction = precond
    residual_inner = residual_dot(residual, precond)
    for iteration in range(ITERS):
        width = direction.shape[1]
        apply_spread = jump(direction, face_index)
        fine_part = jnp.dot(flex_mat, apply_spread, precision=highest)
        local_load = jnp.dot(coupling_mat, apply_spread, precision=highest)
        coarse_rhs = jnp.dot(onehot, local_load, precision=highest)
        coarse_sol = coarse_solve(coarse_rhs, coarse_inverse)
        filled_out = jnp.concatenate([coarse_sol, jnp.zeros((1, width), jnp.float32)], axis=0)
        picked = filled_out[corners]
        correction = lax.dot_general(
            coupling_mat, picked, (((0,), (0,)), ((), ())), precision=highest
        )
        image_dir = jump(fine_part + correction, face_index)
        step_size = residual_inner / lax.psum(inner(direction, image_dir), ("sx", "sy"))
        multipliers = multipliers + step_size * direction
        residual = residual - step_size * image_dir
        if iteration + 1 < ITERS:
            precond = precondition(residual)
            new_dot = residual_dot(residual, precond)
            direction = precond + new_dot / residual_inner * direction
            residual_inner = new_dot
    return (multipliers[None, None], residual[None, None])


def solution(mesh):
    return jax.shard_map(
        shards,
        mesh=mesh,
        in_specs=(
            P("sx", "sy", None, None),
            P("sx", "sy", None, None),
            P("sx", "sy", None, None),
            P("sx", "sy", None, None),
            P("sx", "sy", None),
            P("sx", "sy", None, None),
            P(("sx", "sy"), None),
        ),
        out_specs=(P("sx", "sy", None, None), P("sx", "sy", None, None)),
        check_vma=False,
    )
```

profile of v0, /device:TPU:1, one launch (start us, length us, event | category | flops | bytes accessed | tf_op | source)
XLA Modules:
  0.0 1103.3 jit_solution(2738854772131072380)
XLA Ops:
  8.7 4.6 collective-permute-start
  26.2 4.1 collective-permute-done.3
  30.4 18.0 %gather_fusion = f32[1536,256]{1,0:T(8,128)} fusion(f32[4,384,256]{2,1,0:T(8,128)S(1)} %pad_maximum_fusion, s32[1536]{0:T(1024)S(1)} %reshape.175), kind=kCustom, calls=%fused_computation | custom fusion | bytes 3158016 | tf_op jit(solution)/shard_map/gather | solution.py:24
  51.4 5.1 collective-permute-start.4
  68.1 4.1 collective-permute-done.7
  72.3 18.0 %gather_fusion.1 = f32[1536,256]{1,0:T(8,128)} fusion(f32[4,384,256]{2,1,0:T(8,128)S(1)} %pad_maximum_fusion.1, s32[1536]{0:T(1024)S(1)} %reshape.175), kind=kCustom, calls=%fused_computation.1 | custom fusion | bytes 3158016 | tf_op jit(solution)/shard_map/gather | solution.py:24
  92.1 18.2 %fusion.10 = f32[1536,256]{0,1:T(8,128)S(1)} fusion(f32[1536,256]{1,0:T(8,128)S(1)} %bitcast.126, f32[1,1,1536,1536]{3,2,1,0:T(8,128)} %param.9), kind=kOutput, calls=%fused_computation.23 | convolution fusion | flops 7247757312 | bytes 12582912 | tf_op jit(solution)/shard_map/dot_general | solution.py:51
  110.3 5.9 collective-permute-start.8
  126.9 4.1 collective-permute-done.11
  134.2 18.0 %gather_fusion.2 = f32[1536,256]{1,0:T(8,128)} fusion(f32[4,384,256]{2,1,0:T(8,128)S(1)} %copy.27, s32[1536]{0:T(1024)S(1)} %reshape.175), kind=kCustom, calls=%fused_computation.2 | custom fusion | bytes 3158016 | tf_op jit(solution)/shard_map/gather | solution.py:24
  157.2 6.4 collective-permute-start.12
  181.3 18.0 %gather_fusion.3 = f32[1536,256]{1,0:T(8,128)} fusion(f32[4,384,256]{2,1,0:T(8,128)S(1)} %copy.31, s32[1536]{0:T(1024)S(1)} %reshape.175), kind=kCustom, calls=%fused_computation.3 | custom fusion | bytes 3158016 | tf_op jit(solution)/shard_map/gather | solution.py:24
  203.9 11.6 %fusion.2 = f32[256,1536]{1,0:T(8,128)} fusion(f32[1,1,1536,1536]{3,2,1,0:T(8,128)} %param.8, f32[1536,256]{0,1:T(8,128)S(1)} %copy.32, f32[1536,256]{0,1:T(8,128)S(1)} %get-tuple-element.16), kind=kOutput, calls=%fused_computation.13 | convolution fusion | flops 7248543744 | bytes 14155776 | tf_op jit(solution)/shard_map/dot_general | solution.py:66
  215.4 139.1 %all-reduce.6.cloned.1.call-done = f32[512,256]{1,0:T(8,128)} async-done(((f32[512,256]{1,0:T(8,128)}), f32[512,256]{1,0:T(8,128)}) %all-reduce.6.cloned.1.call-update) | async-done | bytes 524304 | tf_op jit(solution)/shard_map/psum | solution.py:30
  355.9 54.6 %all-gather = f32[128,4,256]{2,1,0:T(4,128)} all-gather(f32[1,4,256]{2,1,0:T(4,128)S(1)} %convolution_bitcast_fusion.1), channel_id=1, replica_groups=mesh['sx'=8,'sy'=16] {'sx','sy'}, dimensions={0}, use_global_device_ids=true | all-gather | bytes 528384 | tf_op jit(solution)/shard_map/all_gather | solution.py:32
  435.2 4.9 collective-permute-done.19
  444.6 18.0 %gather_fusion.5 = f32[1536,256]{1,0:T(8,128)} fusion(f32[4,384,256]{2,1,0:T(8,128)S(1)} %copy.33, s32[1536]{0:T(1024)S(1)} %reshape.175), kind=kCustom, calls=%fused_computation.5 | custom fusion | bytes 3158016 | tf_op jit(solution)/shard_map/gather | solution.py:24
  469.6 66.2 %all-reduce.2 = (f32[256]{0:T(256)S(1)}, f32[256]{0:T(256)S(1)}) all-reduce(f32[256]{0:T(256)S(1)} %get-tuple-element.7, f32[256]{0:T(256)S(1)} %get-tuple-element.6), channel_id=1, replica_groups=mesh['sx'=8,'sy'=16] {'sx','sy'}, use_global_device_ids=true, to_apply=%region_1.0 | all-reduce | flops 512 | bytes 4096 | tf_op jit(solution)/shard_map/psum | solution.py:55
  548.0 4.3 collective-permute-done.21
  562.5 18.0 %gather_fusion.6 = f32[1536,256]{1,0:T(8,128)} fusion(f32[4,384,256]{2,1,0:T(8,128)S(1)} %copy.35, s32[1536]{0:T(1024)S(1)} %reshape.175), kind=kCustom, calls=%fused_computation.6 | custom fusion | bytes 3158016 | tf_op jit(solution)/shard_map/gather | solution.py:24
  583.7 11.3 %fusion.13 = f32[1536,256]{0,1:T(8,128)S(1)} fusion(f32[1,1,1536,1536]{3,2,1,0:T(8,128)} %param.9, f32[1536,256]{0,1:T(8,128)S(1)} %copy-done.5, f32[1536,256]{0,1:T(8,128)} %copy.36), kind=kOutput, calls=%fused_computation.24 | convolution fusion | flops 7248150528 | bytes 14155776 | tf_op jit(solution)/shard_map/dot_general | solution.py:51
  611.5 4.1 collective-permute-done.27
  618.8 18.0 %gather_fusion.7 = f32[1536,256]{1,0:T(8,128)} fusion(f32[4,384,256]{2,1,0:T(8,128)S(1)} %copy.37, s32[1536]{0:T(1024)S(1)} %reshape.175), kind=kCustom, calls=%fused_computation.7 | custom fusion | bytes 3158016 | tf_op jit(solution)/shard_map/gather | solution.py:24
  642.2 69.1 %psum.45 = f32[256]{0:T(256)S(1)} all-reduce(f32[256]{0:T(256)S(1)} %multiply_reduce_fusion.1), channel_id=1, replica_groups=mesh['sx'=8,'sy'=16] {'sx','sy'}, use_global_device_ids=true, to_apply=%region_6.0 | all-reduce | flops 256 | bytes 2048 | tf_op jit(solution)/shard_map/psum | solution.py:55
  723.7 4.3 collective-permute-done.29
  729.7 4.1 collective-permute-done.31
  737.0 18.0 %gather_fusion.8 = f32[1536,256]{1,0:T(8,128)} fusion(f32[4,384,256]{2,1,0:T(8,128)S(1)} %copy.39, s32[1536]{0:T(1024)S(1)} %reshape.175), kind=kCustom, calls=%fused_computation.8 | custom fusion | bytes 3158016 | tf_op jit(solution)/shard_map/gather | solution.py:24
  762.1 12.2 %fusion = f32[256,1536]{1,0:T(8,128)} fusion(f32[1,1,1536,1536]{3,2,1,0:T(8,128)} %param.8, f32[1536,256]{0,1:T(8,128)S(1)} %copy-done.2, f32[1536,256]{0,1:T(8,128)} %copy.40), kind=kOutput, calls=%fused_computation.11 | convolution fusion | flops 7248150528 | bytes 14155776 | tf_op jit(solution)/shard_map/dot_general | solution.py:66
  774.3 135.6 %all-reduce.8.cloned.1.call-done = f32[512,256]{1,0:T(8,128)} async-done(((f32[512,256]{1,0:T(8,128)}), f32[512,256]{1,0:T(8,128)}) %all-reduce.8.cloned.1.call-update) | async-done | bytes 524304 | tf_op jit(solution)/shard_map/psum | solution.py:30
  911.3 54.2 %all-gather.1 = f32[128,4,256]{2,1,0:T(4,128)} all-gather(f32[1,4,256]{2,1,0:T(4,128)S(1)} %convolution_bitcast_fusion), channel_id=1, replica_groups=mesh['sx'=8,'sy'=16] {'sx','sy'}, dimensions={0}, use_global_device_ids=true | all-gather | bytes 528384 | tf_op jit(solution)/shard_map/all_gather | solution.py:32
  995.9 18.0 %gather_fusion.10 = f32[1536,256]{1,0:T(8,128)} fusion(f32[4,384,256]{2,1,0:T(8,128)S(1)} %copy.41, s32[1536]{0:T(1024)S(1)} %reshape.175), kind=kCustom, calls=%fused_computation.10 | custom fusion | bytes 3158016 | tf_op jit(solution)/shard_map/gather | solution.py:24
  1020.4 66.7 %psum.47 = f32[256]{0:T(256)S(1)} all-reduce(f32[256]{0:T(256)S(1)} %get-tuple-element.12), channel_id=1, replica_groups=mesh['sx'=8,'sy'=16] {'sx','sy'}, use_global_device_ids=true, to_apply=%region_9.0 | all-reduce | flops 256 | bytes 2048 | tf_op jit(solution)/shard_map/psum | solution.py:76
  (172 shorter events, 231.1 us)
Async XLA Ops:
  7.2 347.3 %all-reduce.6.cloned.1.call-start = ((), (), s32[]{:S(2)}) async-start(), calls=%async_computation | async-start | bytes 1048576 | tf_op jit(solution)/shard_map/psum | solution.py:30
  8.7 11.4 %collective-permute-start = (f32[384,256]{1,0:T(8,128)S(1)}, f32[384,256]{1,0:T(8,128)S(1)}, u32[]{:S(2)}, u32[]{:S(2)}) collective-permute-start(f32[384,256]{1,0:T(8,128)S(1)} %get-tuple-element.49), channel_id=1, source_target_pairs={{0,16},{16,32},{32,48},{48,64},{64,80},{80,96},{96,112},{1,17},{17... | collective-permute-start | bytes 1179656 | tf_op jit(solution)/shard_map/ppermute | solution.py:12
  13.3 9.4 collective-permute-start.1
  15.2 11.0 collective-permute-start.2
  18.8 11.5 %collective-permute-start.3 = (f32[384,256]{1,0:T(8,128)S(1)}, f32[384,256]{1,0:T(8,128)S(1)}, u32[]{:S(2)}, u32[]{:S(2)}) collective-permute-start(f32[384,256]{1,0:T(8,128)S(1)} %get-tuple-element.52), channel_id=1, source_target_pairs={{1,0},{2,1},{3,2},{4,3},{5,4},{6,5},{7,6},{8,7},{9,8},{10,9},{11,1... | collective-permute-start | bytes 1179656 | tf_op jit(solution)/shard_map/ppermute | solution.py:12
  51.4 11.8 %collective-permute-start.4 = (f32[384,256]{1,0:T(8,128)S(1)}, f32[384,256]{1,0:T(8,128)S(1)}, u32[]{:S(2)}, u32[]{:S(2)}) collective-permute-start(f32[384,256]{1,0:T(8,128)S(1)} %get-tuple-element.45), channel_id=1, source_target_pairs={{0,16},{16,32},{32,48},{48,64},{64,80},{80,96},{96,112},{1,17},{17... | collective-permute-start | bytes 1179656 | tf_op jit(solution)/shard_map/ppermute | solution.py:12
  56.6 9.4 collective-permute-start.5
  58.5 9.6 collective-permute-start.6
  61.9 10.3 collective-permute-start.7
  110.3 13.3 %collective-permute-start.8 = (f32[384,256]{0,1:T(8,128)S(1)}, f32[384,256]{0,1:T(8,128)S(1)}, u32[]{:S(2)}, u32[]{:S(2)}) collective-permute-start(f32[384,256]{0,1:T(8,128)S(1)} %get-tuple-element.41), channel_id=1, source_target_pairs={{0,16},{16,32},{32,48},{48,64},{64,80},{80,96},{96,112},{1,17},{17... | collective-permute-start | bytes 1179656 | tf_op jit(solution)/shard_map/ppermute | solution.py:12
  116.3 9.4 collective-permute-start.9
  157.2 13.8 %collective-permute-start.12 = (f32[384,256]{0,1:T(8,128)S(1)}, f32[384,256]{0,1:T(8,128)S(1)}, u32[]{:S(2)}, u32[]{:S(2)}) collective-permute-start(f32[384,256]{0,1:T(8,128)S(1)} %get-tuple-element.37), channel_id=1, source_target_pairs={{0,16},{16,32},{32,48},{48,64},{64,80},{80,96},{96,112},{1,17},{17... | collective-permute-start | bytes 1179656 | tf_op jit(solution)/shard_map/ppermute | solution.py:12
  163.7 9.4 collective-permute-start.13
  203.8 706.1 %all-reduce.8.cloned.1.call-start = ((), (), s32[]{:S(2)}) async-start(), calls=%async_computation.1 | async-start | bytes 1048576 | tf_op jit(solution)/shard_map/psum | solution.py:30
  419.1 13.7 %collective-permute-start.16 = (f32[384,256]{0,1:T(8,128)}, f32[384,256]{0,1:T(8,128)}, u32[]{:S(2)}, u32[]{:S(2)}) collective-permute-start(f32[384,256]{0,1:T(8,128)} %get-tuple-element.33), channel_id=1, source_target_pairs={{0,16},{16,32},{32,48},{48,64},{64,80},{80,96},{96,112},{1,17},{17... | collective-permute-start | bytes 1179656 | tf_op jit(solution)/shard_map/ppermute | solution.py:12
  421.0 11.8 %collective-permute-start.17 = (f32[384,256]{0,1:T(8,128)}, f32[384,256]{0,1:T(8,128)}, u32[]{:S(2)}, u32[]{:S(2)}) collective-permute-start(f32[384,256]{0,1:T(8,128)} %get-tuple-element.36), channel_id=1, source_target_pairs={{16,0},{32,16},{48,32},{64,48},{80,64},{96,80},{112,96},{17,1},{33... | collective-permute-start | bytes 1179656 | tf_op jit(solution)/shard_map/ppermute | solution.py:12
  424.2 11.1 %collective-permute-start.18 = (f32[384,256]{0,1:T(8,128)}, f32[384,256]{0,1:T(8,128)}, u32[]{:S(2)}, u32[]{:S(2)}) collective-permute-start(f32[384,256]{0,1:T(8,128)} %get-tuple-element.35), channel_id=1, source_target_pairs={{0,1},{1,2},{2,3},{3,4},{4,5},{5,6},{6,7},{7,8},{8,9},{9,10},{10,1... | collective-permute-start | bytes 1179656 | tf_op jit(solution)/shard_map/ppermute | solution.py:12
  426.9 13.2 %collective-permute-start.19 = (f32[384,256]{0,1:T(8,128)}, f32[384,256]{0,1:T(8,128)}, u32[]{:S(2)}, u32[]{:S(2)}) collective-permute-start(f32[384,256]{0,1:T(8,128)} %get-tuple-element.34), channel_id=1, source_target_pairs={{1,0},{2,1},{3,2},{4,3},{5,4},{6,5},{7,6},{8,7},{9,8},{10,9},{11,1... | collective-permute-start | bytes 1179656 | tf_op jit(solution)/shard_map/ppermute | solution.py:12
  542.9 9.4 collective-permute-start.21
  544.8 10.5 collective-permute-start.22
  546.5 12.9 %collective-permute-start.23 = (f32[384,256]{0,1:T(8,128)S(1)}, f32[384,256]{0,1:T(8,128)S(1)}, u32[]{:S(2)}, u32[]{:S(2)}) collective-permute-start(f32[384,256]{0,1:T(8,128)S(1)} %get-tuple-element.30), channel_id=1, source_target_pairs={{1,0},{2,1},{3,2},{4,3},{5,4},{6,5},{7,6},{8,7},{9,8},{10,9},{11,1... | collective-permute-start | bytes 1179656 | tf_op jit(solution)/shard_map/ppermute | solution.py:12
  596.2 9.0 collective-permute-start.24
  599.6 9.4 collective-permute-start.25
  601.5 9.9 collective-permute-start.26
  603.8 11.8 %collective-permute-start.27 = (f32[384,256]{0,1:T(8,128)S(1)}, f32[384,256]{0,1:T(8,128)S(1)}, u32[]{:S(2)}, u32[]{:S(2)}) collective-permute-start(f32[384,256]{0,1:T(8,128)S(1)} %get-tuple-element.26), channel_id=1, source_target_pairs={{1,0},{2,1},{3,2},{4,3},{5,4},{6,5},{7,6},{8,7},{9,8},{10,9},{11,1... | collective-permute-start | bytes 1179656 | tf_op jit(solution)/shard_map/ppermute | solution.py:12
  714.7 9.0 collective-permute-start.28
  718.5 9.4 collective-permute-start.29
  720.5 9.2 collective-permute-start.30
  722.1 11.7 %collective-permute-start.31 = (f32[384,256]{0,1:T(8,128)S(1)}, f32[384,256]{0,1:T(8,128)S(1)}, u32[]{:S(2)}, u32[]{:S(2)}) collective-permute-start(f32[384,256]{0,1:T(8,128)S(1)} %get-tuple-element.22), channel_id=1, source_target_pairs={{1,0},{2,1},{3,2},{4,3},{5,4},{6,5},{7,6},{8,7},{9,8},{10,9},{11,1... | collective-permute-start | bytes 1179656 | tf_op jit(solution)/shard_map/ppermute | solution.py:12
  975.5 9.4 collective-permute-start.33
  977.9 10.7 collective-permute-start.34
  979.9 12.9 %collective-permute-start.35 = (f32[384,256]{0,1:T(8,128)S(1)}, f32[384,256]{0,1:T(8,128)S(1)}, u32[]{:S(2)}, u32[]{:S(2)}) collective-permute-start(f32[384,256]{0,1:T(8,128)S(1)} %get-tuple-element.18), channel_id=1, source_target_pairs={{1,0},{2,1},{3,2},{4,3},{5,4},{6,5},{7,6},{8,7},{9,8},{10,9},{11,1... | collective-permute-start | bytes 1179656 | tf_op jit(solution)/shard_map/ppermute | solution.py:12
  (27 other events, 893.0 us)
Sparse Core Ops, SparseCore 0:
  203.9 150.5 all-reduce.5
  762.2 147.6 all-reduce.7
where the time goes:
time: 1110 us; the launch traced here: 1100 us
  waiting for transfers between devices  359 us (32%)
  blocking collectives  311 us (28%)
  local copies, waits for them, and re-layouts  225 us (20%)
  starting transfers between devices  93.2 us (8%)
  matrix products  65.3 us (6%)
  other arithmetic  34.2 us (3%)
  between operations  15.2 us (1%)
    psum x2, waiting for transfers between devices, coarse_solve(): total = lax.psum(coarse_rhs, ('sx', 'sy'))  275 us
    gather x17, local copies, waits for them, and re-layouts, jump(): matched = received[jnp.arange(4, dtype=jnp.int32)[:, None], face_index]  186 us
    psum x2, blocking collectives, residual_dot(): return lax.psum(inner(residual, precond), ('sx', 'sy'))  135 us
    all_gather x2, blocking collectives, coarse_solve(): return lax.all_gather(mine, ('sx', 'sy'), axis=0, tiled=True)  109 us
    ppermute x36, starting transfers between devices, shifted(): return lax.ppermute(block, axis, route)  93.1 us
    ppermute x36, waiting for transfers between devices, shifted(): return lax.ppermute(block, axis, route)  84.4 us
    psum x1, blocking collectives, shards(): lax.psum(inner(direction, image_dir), ('sx', 'sy'))  66.7 us
    dot_general x2, matrix products, precondition(): operator_applied = jnp.dot(prec_mat, spread, precision=highest)  29.5 us
  transfers between devices with their start and end apart: 38, of which 28 were waited for; matrix products, arithmetic and copies ran while one was open for 3% of the time, Pallas kernels for 0%

commit v1 on v0

--- a/solution.py
+++ b/solution.py
@@ -73,7 +73,9 @@
             coupling_mat, picked, (((0,), (0,)), ((), ())), precision=highest
         )
         image_dir = jump(fine_part + correction, face_index)
-        step_size = residual_inner / lax.psum(inner(direction, image_dir), ("sx", "sy"))
+        step_size = residual_inner / jnp.sum(
+            lax.all_gather(inner(direction, image_dir), ("sx", "sy")), axis=0
+        )
         multipliers = multipliers + step_size * direction
         residual = residual - step_size * image_dir
         if iteration + 1 < ITERS:

time: 1110 us -> 1150 us (1.036)
  blocking collectives: 311 us -> 345 us
    all_gather x0 -> x2, blocking collectives: none -> 104 us  [shards(): lax.all_gather(inner(direction, image_dir), ('sx', 'sy'))]
    psum x1 -> x0, blocking collectives: 66.7 us -> none  [shards(): lax.psum(inner(direction, image_dir), ('sx', 'sy'))]
where the time goes in v1:
time: 1150 us; the launch traced here: 1140 us
  waiting for transfers between devices  359 us (31%)
  blocking collectives  345 us (30%)
  local copies, waits for them, and re-layouts  225 us (20%)
  starting transfers between devices  93 us (8%)
  matrix products  65.4 us (6%)
  other arithmetic  34.6 us (3%)
  between operations  15.2 us (1%)
    psum x2, waiting for transfers between devices, coarse_solve(): total = lax.psum(coarse_rhs, ('sx', 'sy'))  274 us
    gather x17, local copies, waits for them, and re-layouts, jump(): matched = received[jnp.arange(4, dtype=jnp.int32)[:, None], face_index]  186 us
    psum x2, blocking collectives, residual_dot(): return lax.psum(inner(residual, precond), ('sx', 'sy'))  132 us
    all_gather x2, blocking collectives, coarse_solve(): return lax.all_gather(mine, ('sx', 'sy'), axis=0, tiled=True)  109 us
    all_gather x2, blocking collectives, shards(): lax.all_gather(inner(direction, image_dir), ('sx', 'sy'))  104 us
    ppermute x36, starting transfers between devices, shifted(): return lax.ppermute(block, axis, route)  92.9 us
    ppermute x36, waiting for transfers between devices, shifted(): return lax.ppermute(block, axis, route)  85.1 us
    dot_general x2, matrix products, precondition(): operator_applied = jnp.dot(prec_mat, spread, precision=highest)  29.5 us
  transfers between devices with their start and end apart: 38, of which 28 were waited for; matrix products, arithmetic and copies ran while one was open for 3% of the time, Pallas kernels for 0%

profile of v1, /device:TPU:1, one launch (start us, length us, event | category | flops | bytes accessed | tf_op | source)
XLA Modules:
  0.0 1137.9 jit_solution(9506597619995351646)
XLA Ops:
  8.7 4.6 collective-permute-start
  30.4 18.0 %gather_fusion = f32[1536,256]{1,0:T(8,128)} fusion(f32[4,384,256]{2,1,0:T(8,128)S(1)} %pad_maximum_fusion, s32[1536]{0:T(1024)S(1)} %reshape.175), kind=kCustom, calls=%fused_computation | custom fusion | bytes 3158016 | tf_op jit(solution)/shard_map/gather | solution.py:24
  51.4 5.1 collective-permute-start.4
  68.1 4.1 collective-permute-done.7
  72.3 18.0 %gather_fusion.1 = f32[1536,256]{1,0:T(8,128)} fusion(f32[4,384,256]{2,1,0:T(8,128)S(1)} %pad_maximum_fusion.1, s32[1536]{0:T(1024)S(1)} %reshape.175), kind=kCustom, calls=%fused_computation.1 | custom fusion | bytes 3158016 | tf_op jit(solution)/shard_map/gather | solution.py:24
  92.1 18.2 %fusion.10 = f32[1536,256]{0,1:T(8,128)S(1)} fusion(f32[1536,256]{1,0:T(8,128)S(1)} %bitcast.128, f32[1,1,1536,1536]{3,2,1,0:T(8,128)} %param.9), kind=kOutput, calls=%fused_computation.23 | convolution fusion | flops 7247757312 | bytes 12582912 | tf_op jit(solution)/shard_map/dot_general | solution.py:51
  110.4 5.9 collective-permute-start.8
  126.9 4.1 collective-permute-done.11
  134.2 18.0 %gather_fusion.2 = f32[1536,256]{1,0:T(8,128)} fusion(f32[4,384,256]{2,1,0:T(8,128)S(1)} %copy.27, s32[1536]{0:T(1024)S(1)} %reshape.175), kind=kCustom, calls=%fused_computation.2 | custom fusion | bytes 3158016 | tf_op jit(solution)/shard_map/gather | solution.py:24
  157.2 6.4 collective-permute-start.12
  181.3 18.0 %gather_fusion.3 = f32[1536,256]{1,0:T(8,128)} fusion(f32[4,384,256]{2,1,0:T(8,128)S(1)} %copy.31, s32[1536]{0:T(1024)S(1)} %reshape.175), kind=kCustom, calls=%fused_computation.3 | custom fusion | bytes 3158016 | tf_op jit(solution)/shard_map/gather | solution.py:24
  203.9 11.6 %fusion.2 = f32[256,1536]{1,0:T(8,128)} fusion(f32[1,1,1536,1536]{3,2,1,0:T(8,128)} %param.8, f32[1536,256]{0,1:T(8,128)S(1)} %copy.32, f32[1536,256]{0,1:T(8,128)S(1)} %get-tuple-element.14), kind=kOutput, calls=%fused_computation.13 | convolution fusion | flops 7248543744 | bytes 14155776 | tf_op jit(solution)/shard_map/dot_general | solution.py:66
  215.5 139.1 %all-reduce.5.cloned.1.call-done = f32[512,256]{1,0:T(8,128)} async-done(((f32[512,256]{1,0:T(8,128)}), f32[512,256]{1,0:T(8,128)}) %all-reduce.5.cloned.1.call-update) | async-done | bytes 524304 | tf_op jit(solution)/shard_map/psum | solution.py:30
  355.9 54.6 %all-gather.2 = f32[128,4,256]{2,1,0:T(4,128)} all-gather(f32[1,4,256]{2,1,0:T(4,128)S(1)} %convolution_bitcast_fusion.1), channel_id=1, replica_groups=mesh['sx'=8,'sy'=16] {'sx','sy'}, dimensions={0}, use_global_device_ids=true | all-gather | bytes 528384 | tf_op jit(solution)/shard_map/all_gather | solution.py:32
  435.3 4.9 collective-permute-done.19
  444.7 18.0 %gather_fusion.5 = f32[1536,256]{1,0:T(8,128)} fusion(f32[4,384,256]{2,1,0:T(8,128)S(1)} %copy.33, s32[1536]{0:T(1024)S(1)} %reshape.175), kind=kCustom, calls=%fused_computation.5 | custom fusion | bytes 3158016 | tf_op jit(solution)/shard_map/gather | solution.py:24
  469.7 52.0 %all-gather.3 = f32[128,1,256]{2,1,0:T(1,128)S(1)} all-gather(f32[1,1,256]{2,1,0:T(1,128)S(1)} %bitcast.161), channel_id=2, replica_groups=mesh['sx'=8,'sy'=16] {'sx','sy'}, dimensions={0}, use_global_device_ids=true | all-gather | bytes 132096 | tf_op jit(solution)/shard_map/all_gather | solution.py:77
  521.9 64.4 %psum.28 = f32[256]{0:T(256)S(1)} all-reduce(f32[256]{0:T(256)S(1)} %get-tuple-element.7), channel_id=1, replica_groups=mesh['sx'=8,'sy'=16] {'sx','sy'}, use_global_device_ids=true, to_apply=%region_1.0 | all-reduce | flops 256 | bytes 2048 | tf_op jit(solution)/shard_map/psum | solution.py:55
  605.2 4.4 collective-permute-done.23
  612.7 18.0 %gather_fusion.6 = f32[1536,256]{1,0:T(8,128)} fusion(f32[4,384,256]{2,1,0:T(8,128)S(1)} %copy.35, s32[1536]{0:T(1024)S(1)} %reshape.175), kind=kCustom, calls=%fused_computation.6 | custom fusion | bytes 3158016 | tf_op jit(solution)/shard_map/gather | solution.py:24
  633.9 11.3 fusion.13
  661.9 4.1 collective-permute-done.27
  669.2 18.0 %gather_fusion.7 = f32[1536,256]{1,0:T(8,128)} fusion(f32[4,384,256]{2,1,0:T(8,128)S(1)} %copy.37, s32[1536]{0:T(1024)S(1)} %reshape.175), kind=kCustom, calls=%fused_computation.7 | custom fusion | bytes 3158016 | tf_op jit(solution)/shard_map/gather | solution.py:24
  692.7 67.7 %psum.30 = f32[256]{0:T(256)S(1)} all-reduce(f32[256]{0:T(256)S(1)} %multiply_reduce_fusion.1), channel_id=1, replica_groups=mesh['sx'=8,'sy'=16] {'sx','sy'}, use_global_device_ids=true, to_apply=%region_6.0 | all-reduce | flops 256 | bytes 2048 | tf_op jit(solution)/shard_map/psum | solution.py:55
  763.7 4.4 collective-permute-start.28
  772.9 4.6 collective-permute-done.29
  786.5 18.0 %gather_fusion.8 = f32[1536,256]{1,0:T(8,128)} fusion(f32[4,384,256]{2,1,0:T(8,128)S(1)} %copy.39, s32[1536]{0:T(1024)S(1)} %reshape.175), kind=kCustom, calls=%fused_computation.8 | custom fusion | bytes 3158016 | tf_op jit(solution)/shard_map/gather | solution.py:24
  811.7 12.2 %fusion = f32[256,1536]{1,0:T(8,128)} fusion(f32[1,1,1536,1536]{3,2,1,0:T(8,128)} %param.8, f32[1536,256]{0,1:T(8,128)S(1)} %copy-done.2, f32[1536,256]{0,1:T(8,128)} %copy.40), kind=kOutput, calls=%fused_computation.11 | convolution fusion | flops 7248150528 | bytes 14155776 | tf_op jit(solution)/shard_map/dot_general | solution.py:66
  823.9 135.1 %all-reduce.7.cloned.1.call-done = f32[512,256]{1,0:T(8,128)} async-done(((f32[512,256]{1,0:T(8,128)}), f32[512,256]{1,0:T(8,128)}) %all-reduce.7.cloned.1.call-update) | async-done | bytes 524304 | tf_op jit(solution)/shard_map/psum | solution.py:30
  960.4 54.2 %all-gather.4 = f32[128,4,256]{2,1,0:T(4,128)} all-gather(f32[1,4,256]{2,1,0:T(4,128)S(1)} %convolution_bitcast_fusion), channel_id=1, replica_groups=mesh['sx'=8,'sy'=16] {'sx','sy'}, dimensions={0}, use_global_device_ids=true | all-gather | bytes 528384 | tf_op jit(solution)/shard_map/all_gather | solution.py:32
  1045.2 17.9 %gather_fusion.10 = f32[1536,256]{1,0:T(8,128)} fusion(f32[4,384,256]{2,1,0:T(8,128)S(1)} %copy.41, s32[1536]{0:T(1024)S(1)} %reshape.175), kind=kCustom, calls=%fused_computation.10 | custom fusion | bytes 3158016 | tf_op jit(solution)/shard_map/gather | solution.py:24
  1069.6 52.0 %all-gather.5 = f32[128,1,256]{2,1,0:T(1,128)S(1)} all-gather(f32[1,1,256]{2,1,0:T(1,128)S(1)} %bitcast.162), channel_id=3, replica_groups=mesh['sx'=8,'sy'=16] {'sx','sy'}, dimensions={0}, use_global_device_ids=true | all-gather | bytes 132096 | tf_op jit(solution)/shard_map/all_gather | solution.py:77
  (175 shorter events, 235.5 us)
Async XLA Ops:
  7.2 347.4 %all-reduce.5.cloned.1.call-start = ((), (), s32[]{:S(2)}) async-start(), calls=%async_computation | async-start | bytes 1048576 | tf_op jit(solution)/shard_map/psum | solution.py:30
  8.7 11.4 %collective-permute-start = (f32[384,256]{1,0:T(8,128)S(1)}, f32[384,256]{1,0:T(8,128)S(1)}, u32[]{:S(2)}, u32[]{:S(2)}) collective-permute-start(f32[384,256]{1,0:T(8,128)S(1)} %get-tuple-element.47), channel_id=1, source_target_pairs={{0,16},{16,32},{32,48},{48,64},{64,80},{80,96},{96,112},{1,17},{17... | collective-permute-start | bytes 1179656 | tf_op jit(solution)/shard_map/ppermute | solution.py:12
  13.3 9.4 collective-permute-start.1
  15.2 11.0 collective-permute-start.2
  18.8 11.5 %collective-permute-start.3 = (f32[384,256]{1,0:T(8,128)S(1)}, f32[384,256]{1,0:T(8,128)S(1)}, u32[]{:S(2)}, u32[]{:S(2)}) collective-permute-start(f32[384,256]{1,0:T(8,128)S(1)} %get-tuple-element.50), channel_id=1, source_target_pairs={{1,0},{2,1},{3,2},{4,3},{5,4},{6,5},{7,6},{8,7},{9,8},{10,9},{11,1... | collective-permute-start | bytes 1179656 | tf_op jit(solution)/shard_map/ppermute | solution.py:12
  51.4 11.8 %collective-permute-start.4 = (f32[384,256]{1,0:T(8,128)S(1)}, f32[384,256]{1,0:T(8,128)S(1)}, u32[]{:S(2)}, u32[]{:S(2)}) collective-permute-start(f32[384,256]{1,0:T(8,128)S(1)} %get-tuple-element.43), channel_id=1, source_target_pairs={{0,16},{16,32},{32,48},{48,64},{64,80},{80,96},{96,112},{1,17},{17... | collective-permute-start | bytes 1179656 | tf_op jit(solution)/shard_map/ppermute | solution.py:12
  56.6 9.4 collective-permute-start.5
  58.5 9.6 collective-permute-start.6
  61.9 10.3 collective-permute-start.7
  110.4 13.3 %collective-permute-start.8 = (f32[384,256]{0,1:T(8,128)S(1)}, f32[384,256]{0,1:T(8,128)S(1)}, u32[]{:S(2)}, u32[]{:S(2)}) collective-permute-start(f32[384,256]{0,1:T(8,128)S(1)} %get-tuple-element.39), channel_id=1, source_target_pairs={{0,16},{16,32},{32,48},{48,64},{64,80},{80,96},{96,112},{1,17},{17... | collective-permute-start | bytes 1179656 | tf_op jit(solution)/shard_map/ppermute | solution.py:12
  116.3 9.4 collective-permute-start.9
  122.2 8.9 collective-permute-start.11
  157.2 13.8 %collective-permute-start.12 = (f32[384,256]{0,1:T(8,128)S(1)}, f32[384,256]{0,1:T(8,128)S(1)}, u32[]{:S(2)}, u32[]{:S(2)}) collective-permute-start(f32[384,256]{0,1:T(8,128)S(1)} %get-tuple-element.35), channel_id=1, source_target_pairs={{0,16},{16,32},{32,48},{48,64},{64,80},{80,96},{96,112},{1,17},{17... | collective-permute-start | bytes 1179656 | tf_op jit(solution)/shard_map/ppermute | solution.py:12
  163.7 9.4 collective-permute-start.13
  203.8 755.2 %all-reduce.7.cloned.1.call-start = ((), (), s32[]{:S(2)}) async-start(), calls=%async_computation.1 | async-start | bytes 1048576 | tf_op jit(solution)/shard_map/psum | solution.py:30
  419.2 13.7 %collective-permute-start.16 = (f32[384,256]{0,1:T(8,128)}, f32[384,256]{0,1:T(8,128)}, u32[]{:S(2)}, u32[]{:S(2)}) collective-permute-start(f32[384,256]{0,1:T(8,128)} %get-tuple-element.31), channel_id=1, source_target_pairs={{0,16},{16,32},{32,48},{48,64},{64,80},{80,96},{96,112},{1,17},{17... | collective-permute-start | bytes 1179656 | tf_op jit(solution)/shard_map/ppermute | solution.py:12
  421.1 11.8 %collective-permute-start.17 = (f32[384,256]{0,1:T(8,128)}, f32[384,256]{0,1:T(8,128)}, u32[]{:S(2)}, u32[]{:S(2)}) collective-permute-start(f32[384,256]{0,1:T(8,128)} %get-tuple-element.34), channel_id=1, source_target_pairs={{16,0},{32,16},{48,32},{64,48},{80,64},{96,80},{112,96},{17,1},{33... | collective-permute-start | bytes 1179656 | tf_op jit(solution)/shard_map/ppermute | solution.py:12
  424.3 11.0 collective-permute-start.18
  427.0 13.2 %collective-permute-start.19 = (f32[384,256]{0,1:T(8,128)}, f32[384,256]{0,1:T(8,128)}, u32[]{:S(2)}, u32[]{:S(2)}) collective-permute-start(f32[384,256]{0,1:T(8,128)} %get-tuple-element.32), channel_id=1, source_target_pairs={{1,0},{2,1},{3,2},{4,3},{5,4},{6,5},{7,6},{8,7},{9,8},{10,9},{11,1... | collective-permute-start | bytes 1179656 | tf_op jit(solution)/shard_map/ppermute | solution.py:12
  592.6 9.4 collective-permute-start.21
  594.5 10.7 collective-permute-start.22
  596.6 12.9 %collective-permute-start.23 = (f32[384,256]{0,1:T(8,128)S(1)}, f32[384,256]{0,1:T(8,128)S(1)}, u32[]{:S(2)}, u32[]{:S(2)}) collective-permute-start(f32[384,256]{0,1:T(8,128)S(1)} %get-tuple-element.28), channel_id=1, source_target_pairs={{1,0},{2,1},{3,2},{4,3},{5,4},{6,5},{7,6},{8,7},{9,8},{10,9},{11,1... | collective-permute-start | bytes 1179656 | tf_op jit(solution)/shard_map/ppermute | solution.py:12
  649.5 9.4 collective-permute-start.25
  651.5 10.4 collective-permute-start.26
  653.9 12.2 %collective-permute-start.27 = (f32[384,256]{0,1:T(8,128)S(1)}, f32[384,256]{0,1:T(8,128)S(1)}, u32[]{:S(2)}, u32[]{:S(2)}) collective-permute-start(f32[384,256]{0,1:T(8,128)S(1)} %get-tuple-element.24), channel_id=1, source_target_pairs={{1,0},{2,1},{3,2},{4,3},{5,4},{6,5},{7,6},{8,7},{9,8},{10,9},{11,1... | collective-permute-start | bytes 1179656 | tf_op jit(solution)/shard_map/ppermute | solution.py:12
  763.7 9.2 collective-permute-start.28
  768.1 9.4 collective-permute-start.29
  770.1 9.2 collective-permute-start.30
  771.4 12.0 %collective-permute-start.31 = (f32[384,256]{0,1:T(8,128)S(1)}, f32[384,256]{0,1:T(8,128)S(1)}, u32[]{:S(2)}, u32[]{:S(2)}) collective-permute-start(f32[384,256]{0,1:T(8,128)S(1)} %get-tuple-element.20), channel_id=1, source_target_pairs={{1,0},{2,1},{3,2},{4,3},{5,4},{6,5},{7,6},{8,7},{9,8},{10,9},{11,1... | collective-permute-start | bytes 1179656 | tf_op jit(solution)/shard_map/ppermute | solution.py:12
  1024.7 9.4 collective-permute-start.33
  1027.1 10.8 collective-permute-start.34
  1029.1 12.9 %collective-permute-start.35 = (f32[384,256]{0,1:T(8,128)S(1)}, f32[384,256]{0,1:T(8,128)S(1)}, u32[]{:S(2)}, u32[]{:S(2)}) collective-permute-start(f32[384,256]{0,1:T(8,128)S(1)} %get-tuple-element.16), channel_id=1, source_target_pairs={{1,0},{2,1},{3,2},{4,3},{5,4},{6,5},{7,6},{8,7},{9,8},{10,9},{11,1... | collective-permute-start | bytes 1179656 | tf_op jit(solution)/shard_map/ppermute | solution.py:12
  (27 other events, 892.3 us)
Sparse Core Ops, SparseCore 0:
  204.0 150.5 all-reduce.4
  811.8 147.1 all-reduce.6
